TPU v7x, 32 devices: a whole 2x2x4 slice. The times are simulated.
32 devices in a mesh: node: 8 (over z, x), mp: 4 (over y, core).
Axes of the slice: x: 2, y: 2, z: 4, core: 2. Of those that a mesh axis runs over, the one named last changes fastest.
Arguments:
- queries: bfloat16 [32, 64, 128], P('node', 'mp'), may hold values from -8 to 8
- root_keys: bfloat16 [16384, 8, 128], P('node', 'mp'), may hold values from -6 to 6
- root_values: bfloat16 [16384, 8, 128], P('node', 'mp'), may hold values from -6 to 6
- mid_keys: bfloat16 [8, 1024, 8, 128], P('node', None, 'mp'), may hold values from -6 to 6
- mid_values: bfloat16 [8, 1024, 8, 128], P('node', None, 'mp'), may hold values from -6 to 6
- leaf_keys: bfloat16 [32, 256, 8, 128], P('node', None, 'mp'), may hold values from -6 to 6
- leaf_values: bfloat16 [32, 256, 8, 128], P('node', None, 'mp'), may hold values from -6 to 6
- mid_length: int32 [8], replicated, may hold values from 1 to 1024
- leaf_length: int32 [32], P('node'), may hold values from 1 to 256
- branch_mid: int32 [32, 1], replicated, may hold values from 0 to 7; in each aligned block of 32 rows (0 to 31, 32 to 63, ...) at most 8 rows name the same one
- residual: bfloat16 [32, 8192], P(None, 'node'), may hold values from -6 to 6
- norm_gain: float32 [8192], P('node'), may hold values from 0.5 to 1.5
- out_weight: bfloat16 [8192, 8192], P('mp', 'node'), may hold values from -0.0625 to 0.0625
- gate_weight: bfloat16 [8192, 28672], P('node', 'mp'), may hold values from -0.0625 to 0.0625
- up_weight: bfloat16 [8192, 28672], P('node', 'mp'), may hold values from -0.0625 to 0.0625
- down_weight: bfloat16 [28672, 8192], P('mp', 'node'), may hold values from -0.03125 to 0.03125
Outputs:
- layer_out: bfloat16 [32, 8192], P('mp', 'node')
Inputs may be any that keep to these rules, and one draw needn't show every extreme that they name: `branch_mid`: every inner tree node lies on the path of 1 to 8 branches, and some node on exactly 8.
All inputs are finite; a program needn't handle non-finite values.
Results may differ from a plain program's by a relative error of at most 0.015.
Values may be sent and summed in bfloat16 or wider, within the bound.
A program may use at most 128 MiB of HBM per device.

v0:
```python
import jax
import jax.numpy as jnp
from jax import lax
from jax.sharding import PartitionSpec as P

D = 8192
CAP = 8
masked_score = -1e30
norm_eps = 1e-05


def partial_scores(grouped, key_block, value_block, usable, scaling):
    scores = (
        jnp.einsum("bkgd,lkd->bkgl", grouped, key_block, preferred_element_type=jnp.float32)
        * scaling
    )
    masking = usable[:, None, None, :]
    scores = jnp.where(masking, scores, masked_score)
    highest = jnp.max(scores, axis=-1)
    weights = jnp.where(masking, jnp.exp(scores - highest[..., None]), 0.0)
    weighted = jnp.einsum(
        "bkgl,lkd->bkgd",
        weights.astype(jnp.bfloat16),
        value_block,
        preferred_element_type=jnp.float32,
    )
    return (highest, jnp.sum(weights, axis=-1), weighted)


def combine_parts(earlier, later):
    highest = jnp.maximum(earlier[0], later[0])
    first_factor = jnp.exp(earlier[0] - highest)
    second_factor = jnp.exp(later[0] - highest)
    totals = earlier[1] * first_factor + later[1] * second_factor
    weighted = earlier[2] * first_factor[..., None] + later[2] * second_factor[..., None]
    return (highest, totals, weighted)


def on_device(
    queries,
    root_keys,
    root_values,
    mid_keys,
    mid_values,
    leaf_keys,
    leaf_values,
    mid_length,
    leaf_length,
    branch_mid,
    residual,
    norm_gain,
    out_weight,
    gate_weight,
    up_weight,
    down_weight,
):
    owned = queries.shape[0]
    local_heads = queries.shape[1]
    head_size = queries.shape[2]
    local_groups = root_keys.shape[1]
    group_size = local_heads // local_groups
    scaling = head_size ** (-0.5)
    node_count = lax.axis_size("node")
    gathered = lax.all_gather(queries, "node", axis=0, tiled=True)
    every_branch = gathered.shape[0]
    grouped = gathered.reshape(every_branch, local_groups, group_size, head_size)
    root_usable = jnp.ones((every_branch, root_keys.shape[0]), dtype=bool)
    root_part = partial_scores(grouped, root_keys, root_values, root_usable, scaling)
    local_mids = mid_keys.shape[0]
    node_ids = lax.axis_index("node") * local_mids + jnp.arange(local_mids, dtype=jnp.int32)
    routing = branch_mid[:, 0]
    matching = routing[None, :] == node_ids[:, None]
    ranking = jnp.cumsum(matching.astype(jnp.int32), axis=1) - 1
    selected = matching[:, None, :] & (
        ranking[:, None, :] == jnp.arange(CAP, dtype=jnp.int32)[None, :, None]
    )
    picked = jnp.einsum(
        "ncb,bkgd->nckgd",
        selected.astype(jnp.bfloat16),
        grouped,
        preferred_element_type=jnp.float32,
    ).astype(jnp.bfloat16)
    slot_index = jnp.arange(mid_keys.shape[1])

    def node_partial(inputs):
        node_queries, node_keys, node_values, node_id = inputs
        usable = jnp.broadcast_to(
            slot_index[None, :] < mid_length[node_id], (CAP, slot_index.shape[0])
        )
        return partial_scores(node_queries, node_keys, node_values, usable, scaling)

    node_high, node_totals, node_weighted = lax.map(
        node_partial, (picked, mid_keys, mid_values, node_ids)
    )
    chosen = selected.astype(jnp.float32)
    covered = jnp.sum(chosen, axis=(0, 1))
    back_high = (
        jnp.einsum("ncb,nckg->bkg", chosen, node_high, precision=lax.Precision.HIGHEST)
        + ((1.0 - covered) * masked_score)[:, None, None]
    )
    back_totals = jnp.einsum("ncb,nckg->bkg", chosen, node_totals, precision=lax.Precision.HIGHEST)
    back_weighted = jnp.einsum(
        "ncb,nckgd->bkgd", chosen, node_weighted, precision=lax.Precision.HIGHEST
    )
    shared_part = combine_parts(root_part, (back_high, back_totals, back_weighted))
    peaks, totals, weighted = (
        lax.all_to_all(shared_part[0], "node", split_axis=0, concat_axis=0, tiled=True),
        lax.all_to_all(shared_part[1], "node", split_axis=0, concat_axis=0, tiled=True),
        lax.all_to_all(shared_part[2], "node", split_axis=0, concat_axis=0, tiled=True),
    )
    peaks = peaks.reshape(node_count, owned, local_groups, group_size)
    totals = totals.reshape(node_count, owned, local_groups, group_size)
    weighted = weighted.reshape(node_count, owned, local_groups, group_size, head_size)
    highest = jnp.max(peaks, axis=0)
    factor = jnp.exp(peaks - highest[None])
    merged = (
        highest,
        jnp.sum(totals * factor, axis=0),
        jnp.sum(weighted * factor[..., None], axis=0),
    )
    own_grouped = queries.reshape(owned, local_groups, group_size, head_size)
    leaf_scores = (
        jnp.einsum("bkgd,blkd->bkgl", own_grouped, leaf_keys, preferred_element_type=jnp.float32)
        * scaling
    )
    leaf_usable = (jnp.arange(leaf_keys.shape[1])[None, :] < leaf_length[:, None])[:, None, None, :]
    leaf_scores = jnp.where(leaf_usable, leaf_scores, masked_score)
    leaf_peak = jnp.max(leaf_scores, axis=-1)
    leaf_weights = jnp.where(leaf_usable, jnp.exp(leaf_scores - leaf_peak[..., None]), 0.0)
    leaf_weighted = jnp.einsum(
        "bkgl,blkd->bkgd",
        leaf_weights.astype(jnp.bfloat16),
        leaf_values,
        preferred_element_type=jnp.float32,
    )
    final_part = combine_parts(merged, (leaf_peak, jnp.sum(leaf_weights, axis=-1), leaf_weighted))
    attended = (
        (final_part[2] / final_part[1][..., None])
        .reshape(owned, local_heads * head_size)
        .astype(jnp.bfloat16)
    )
    projected = jnp.dot(
        lax.all_gather(attended, "node", axis=0, tiled=True),
        out_weight,
        preferred_element_type=jnp.float32,
    )
    projected = lax.psum(projected.astype(jnp.bfloat16), "mp").astype(jnp.float32)
    stream = residual.astype(jnp.float32) + projected
    squares = lax.psum(jnp.sum(stream * stream, axis=1), "node")
    normed = (stream * lax.rsqrt(squares[:, None] / D + norm_eps) * norm_gain[None, :]).astype(
        jnp.bfloat16
    )
    out_rows = every_branch // lax.axis_size("mp")
    gate, upward = (
        lax.psum(
            jnp.dot(normed, gate_weight, preferred_element_type=jnp.float32).astype(jnp.bfloat16),
            "node",
        ).astype(jnp.float32),
        lax.psum(
            jnp.dot(normed, up_weight, preferred_element_type=jnp.float32).astype(jnp.bfloat16),
            "node",
        ).astype(jnp.float32),
    )
    act = (jax.nn.silu(gate) * upward).astype(jnp.bfloat16)
    mlp_rows = lax.psum_scatter(
        jnp.dot(act, down_weight, preferred_element_type=jnp.float32).astype(jnp.bfloat16),
        "mp",
        scatter_dimension=0,
        tiled=True,
    ).astype(jnp.float32)
    stream_rows = lax.dynamic_slice_in_dim(stream, lax.axis_index("mp") * out_rows, out_rows, 0)
    return (stream_rows + mlp_rows).astype(jnp.bfloat16)


def solution(mesh):
    in_specs = (
        P("node", "mp", None),
        P("node", "mp", None),
        P("node", "mp", None),
        P("node", None, "mp", None),
        P("node", None, "mp", None),
        P("node", None, "mp", None),
        P("node", None, "mp", None),
        P(),
        P("node"),
        P(),
        P(None, "node"),
        P("node"),
        P("mp", "node"),
        P("node", "mp"),
        P("node", "mp"),
        P("mp", "node"),
    )
    out_specs = P("mp", "node")
    return jax.shard_map(
        on_device, mesh=mesh, in_specs=in_specs, out_specs=out_specs, check_vma=False
    )
```

profile of v0, /device:TPU:0, one launch (start us, length us, event | category | flops | bytes accessed | tf_op | source)
XLA Modules:
  0.0 297.3 jit_solution(1106771095615868161)
XLA Ops:
  6.5 0.0 copy-start
  6.5 1.3 dynamic_slice.18
  7.9 0.6 iota_compare_fusion.2
  8.5 0.7 compare_bitcast_fusion
  9.2 0.1 copy.97
  9.3 0.1 reduce-window.7
  9.3 0.1 add_reduce_fusion
  9.5 32.5 %all_gather.6 = bf16[32,16,128]{2,1,0:T(8,128)(2,1)S(1)} all-gather(bf16[4,16,128]{2,1,0:T(8,128)(2,1)} %param.16), channel_id=1, replica_groups=mesh['node'=8,'mp'=4] {'node'}, dimensions={0}, use_global_device_ids=true | all-gather | bytes 147456 | tf_op jit(solution)/shard_map/all_gather | solution.py:64
  42.1 0.1 convolution_convert_fusion.4
  42.2 1.4 fusion.79
  43.6 0.1 copy.100
  43.7 0.2 fusion.37
  43.9 0.1 copy.114
  44.0 0.0 copy-start.7
  44.0 2.1 bitcast_reduce_fusion
  46.1 0.0 copy-start.1
  46.1 0.1 subtract_exponential_fusion.1
  46.2 1.8 copy-done.1
  48.0 0.8 fusion.1
  48.9 0.1 fusion.22
  49.0 0.7 copy.115
  49.7 5.5 %all-to-all-start.2 = ((f32[32,2,8]{2,1,0:T(2,128)}), f32[32,2,8]{2,1,0:T(2,128)S(1)}, u32[]{:S(2)}, u32[]{:S(2)}) async-start(f32[32,2,8]{2,1,0:T(2,128)} %copy.115), calls=%async_computation.2 | async-start | bytes 65536 | tf_op jit(solution)/shard_map/all_to_all | solution.py:108
  55.1 0.0 copy-done.9
  55.1 0.1 iota_compare_fusion
  55.2 0.0 copy-done.7
  55.2 0.3 convolution_bitcast_fusion
  55.5 0.0 copy-done
  55.5 0.0 copy-start.8
  55.5 3.3 %fusion.13 = f32[32,2,8,128]{3,0,2,1:T(8,128)S(1)} fusion(f32[2,2048,32,8]{1,2,3,0:T(8,128)} %copy-done.1, f32[32,2,8]{0,2,1:T(8,128)S(1)} %get-tuple-element.48, bf16[2048,2,128,1]{2,1,0,3:T(2,128)(2,1)S(1)} %bitcast.75, f32[32,2,8]{0,2,1:T(8,128)S(1)} %subtract_exponential_fusion.2), kind=kOutput, calls=%fused_computation.16 | convolution fusion | flops 271646720 | bytes 5509120 | tf_op jit(solution)/shard_map/bkgl,lkd->bkgd/dot_general | solution.py:21
  58.8 0.0 copy-done.4
  58.8 0.0 copy-done.6
  58.8 0.3 fusion.80
  59.2 0.7 copy.104
  59.9 2.0 all-to-all-done.2
  61.8 4.2 %all-to-all-start.1 = ((f32[32,2,8]{2,1,0:T(2,128)}), f32[32,2,8]{2,1,0:T(2,128)S(1)}, u32[]{:S(2)}, u32[]{:S(2)}) async-start(f32[32,2,8]{2,1,0:T(2,128)} %copy.104), calls=%async_computation.1 | async-start | bytes 65536 | tf_op jit(solution)/shard_map/all_to_all | solution.py:107
  66.0 0.3 fusion.12
  66.3 0.8 copy.103
  67.2 5.5 %all-to-all-done.1 = f32[32,2,8]{2,1,0:T(2,128)S(1)} async-done(((f32[32,2,8]{2,1,0:T(2,128)}), f32[32,2,8]{2,1,0:T(2,128)S(1)}, u32[]{:S(2)}, u32[]{:S(2)}) %all-to-all-start.1) | async-done | bytes 2080 | tf_op jit(solution)/shard_map/all_to_all | solution.py:107
  72.7 3.4 %all-to-all-start = ((f32[32,2,8,128]{3,2,1,0:T(8,128)}), f32[32,2,8,128]{3,2,1,0:T(8,128)S(1)}, u32[]{:S(2)}, u32[]{:S(2)}) async-start(f32[32,2,8,128]{3,2,1,0:T(8,128)} %copy.103), calls=%async_computation | async-start | bytes 524288 | tf_op jit(solution)/shard_map/all_to_all | solution.py:109
  76.1 0.0 all-reduce.4.cloned.1.call-start
  76.1 0.2 fusion.45
  76.5 7.9 %all-to-all-done = f32[32,2,8,128]{3,2,1,0:T(8,128)S(1)} async-done(((f32[32,2,8,128]{3,2,1,0:T(8,128)}), f32[32,2,8,128]{3,2,1,0:T(8,128)S(1)}, u32[]{:S(2)}, u32[]{:S(2)}) %all-to-all-start) | async-done | bytes 262176 | tf_op jit(solution)/shard_map/all_to_all | solution.py:109
  84.3 0.1 fusion.40
  84.5 0.0 copy-done.8
  84.5 0.2 fusion.19
  84.8 30.6 %all-gather = bf16[8,4,2048]{2,1,0:T(4,128)(2,1)S(1)} all-gather(bf16[1,4,2048]{2,1,0:T(4,128)(2,1)S(1)} %reshape.273), channel_id=1, replica_groups=mesh['node'=8,'mp'=4] {'node'}, dimensions={0}, use_global_device_ids=true | all-gather | bytes 147456 | tf_op jit(solution)/shard_map/all_gather | solution.py:143
  115.4 3.6 %convolution_convert_fusion.3 = bf16[32,1024]{1,0:T(8,128)(2,1)} fusion(bf16[32,2048]{1,0:T(8,128)(2,1)S(1)} %reshape.274, bf16[2048,1024]{1,0:T(8,128)(2,1)} %param.28), kind=kOutput, calls=%fused_computation.20 | convolution fusion | flops 134250496 | bytes 4390912 | tf_op jit(solution)/shard_map/dot_general | solution.py:142
  119.0 0.0 all-reduce.4.cloned.1.call-update
  119.0 0.0 all-reduce.6.cloned.1.call-start
  119.1 30.0 %all-reduce.4.cloned.1.call-done = bf16[32,1024]{1,0:T(8,128)(2,1)} async-done(((bf16[32,1024]{1,0:T(8,128)(2,1)}), bf16[32,1024]{1,0:T(8,128)(2,1)}) %all-reduce.4.cloned.1.call-update) | async-done | bytes 65552 | tf_op jit(solution)/shard_map/psum | solution.py:147
  149.1 0.0 copy-done.2
  149.1 1.0 convert_add_fusion
  150.1 21.4 %psum.29 = f32[32]{0:T(128)S(1)} all-reduce(f32[32]{0:T(128)S(1)} %get-tuple-element.45), channel_id=1, replica_groups=mesh['node'=8,'mp'=4] {'node'}, use_global_device_ids=true, to_apply=%region_13.14 | all-reduce | flops 32 | bytes 256 | tf_op jit(solution)/shard_map/psum | solution.py:149
  171.4 0.0 copy-done.5
  171.4 8.7 %convolution_convert_fusion = bf16[32,7168]{1,0:T(8,128)(2,1)} fusion(bf16[1024,7168]{1,0:T(8,128)(2,1)} %param.30, f32[1024]{0:T(1024)S(1)} %copy-done.5, f32[32]{0:T(128)S(1)} %add_rsqrt_fusion, bf16[32,1024]{1,0:T(8,128)(2,1)} %all-reduce.4.cloned.1.call-done, bf16[32,1024]{1,0:T(8,128)(2,1)S(1)} %copy-done.2), kind=kOutput, calls=%fused_computation | convolution fusion | flops 470188032 | bytes 15274112 | tf_op jit(solution)/shard_map/dot_general | solution.py:160
  180.1 0.0 copy-done.3
  180.1 8.6 %convolution_convert_fusion.1 = bf16[32,7168]{1,0:T(8,128)(2,1)} fusion(bf16[1024,7168]{1,0:T(8,128)(2,1)} %param.29, f32[1024]{0:T(1024)S(1)} %copy-done.5, f32[32]{0:T(128)S(1)} %add_rsqrt_fusion, bf16[32,1024]{1,0:T(8,128)(2,1)S(1)} %copy-done.3, bf16[32,1024]{1,0:T(8,128)(2,1)S(1)} %copy-done.2), kind=kOutput, calls=%fused_computation.1 | convolution fusion | flops 470188032 | bytes 15274112 | tf_op jit(solution)/shard_map/dot_general | solution.py:156
  188.7 0.0 all-reduce.6.cloned.1.call-update
  188.7 0.0 reduce-scatter.2.cloned.1.call-start
  188.8 73.1 %all-reduce.6.cloned.1.call-done = (bf16[32,7168]{1,0:T(8,128)(2,1)}, bf16[32,7168]{1,0:T(8,128)(2,1)}) async-done(((bf16[32,7168]{1,0:T(8,128)(2,1)}, bf16[32,7168]{1,0:T(8,128)(2,1)}), (bf16[32,7168]{1,0:T(8,128)(2,1)}, bf16[32,7168]{1,0:T(8,128)(2,1)})) %all-reduce.6.cloned.1.call-update) | async-done | bytes 917520 | tf_op jit(solution)/shard_map/psum | solution.py:159
  261.8 8.7 %convolution_convert_fusion.2 = bf16[32,1024]{1,0:T(8,128)(2,1)} fusion(bf16[7168,1024]{1,0:T(8,128)(2,1)} %param.31, bf16[32,7168]{1,0:T(8,128)(2,1)} %get-tuple-element.23, bf16[32,7168]{1,0:T(8,128)(2,1)} %get-tuple-element.24), kind=kOutput, calls=%fused_computation.19 | convolution fusion | flops 471629824 | bytes 15663104 | tf_op jit(solution)/shard_map/dot_general | solution.py:166
  270.6 0.0 reduce-scatter.2.cloned.1.call-update
  270.6 18.8 %reduce-scatter.2.cloned.1.call-done = bf16[8,1024]{1,0:T(8,128)(2,1)} async-done(((bf16[32,1024]{1,0:T(8,128)(2,1)}), bf16[8,1024]{1,0:T(8,128)(2,1)}) %reduce-scatter.2.cloned.1.call-update) | async-done | bytes 16400 | tf_op jit(solution)/shard_map/reduce_scatter | solution.py:165
  289.4 1.3 add_convert_fusion
  (21 shorter events, 0.2 us)
Async XLA Ops:
  6.5 49.0 %copy-start = (bf16[2048,2,128]{2,1,0:T(2,128)(2,1)S(1)}, bf16[2048,2,128]{2,1,0:T(2,128)(2,1)}, u32[]{:S(2)}) copy-start(bf16[2048,2,128]{2,1,0:T(2,128)(2,1)} %param.18) | copy-start | bytes 3145732
  44.0 11.1 %copy-start.9 = (s32[4]{0:T(128)S(1)}, s32[4]{0:T(128)}, u32[]{:S(2)}) copy-start(s32[4]{0:T(128)} %param.24) | copy-start | bytes 52
  44.0 11.2 %copy-start.7 = (bf16[1,1024,2,128]{3,2,1,0:T(2,128)(2,1)S(1)}, bf16[1,1024,2,128]{3,2,1,0:T(2,128)(2,1)}, u32[]{:S(2)}) copy-start(bf16[1,1024,2,128]{3,2,1,0:T(2,128)(2,1)} %param.20) | copy-start | bytes 1572868
  46.1 1.9 copy-start.1
  48.9 10.0 %copy-start.4 = (bf16[4,256,2,128]{3,2,1,0:T(2,128)(2,1)S(1)}, bf16[4,256,2,128]{3,2,1,0:T(2,128)(2,1)}, u32[]{:S(2)}) copy-start(bf16[4,256,2,128]{3,2,1,0:T(2,128)(2,1)} %param.21) | copy-start | bytes 1572868
  48.9 10.0 %copy-start.6 = (bf16[4,16,128]{2,1,0:T(8,128)(2,1)S(1)}, bf16[4,16,128]{2,1,0:T(8,128)(2,1)}, u32[]{:S(2)}) copy-start(bf16[4,16,128]{2,1,0:T(8,128)(2,1)} %param.16) | copy-start | bytes 49156
  49.7 12.1 %all-to-all-start.2 = ((f32[32,2,8]{2,1,0:T(2,128)}), f32[32,2,8]{2,1,0:T(2,128)S(1)}, u32[]{:S(2)}, u32[]{:S(2)}) async-start(f32[32,2,8]{2,1,0:T(2,128)} %copy.115), calls=%async_computation.2 | async-start | bytes 65536 | tf_op jit(solution)/shard_map/all_to_all | solution.py:108
  55.5 29.0 %copy-start.8 = (bf16[4,256,2,128]{3,2,1,0:T(2,128)(2,1)S(1)}, bf16[4,256,2,128]{3,2,1,0:T(2,128)(2,1)}, u32[]{:S(2)}) copy-start(bf16[4,256,2,128]{3,2,1,0:T(2,128)(2,1)} %param.22) | copy-start | bytes 1572868
  59.9 89.2 %copy-start.2 = (bf16[32,1024]{1,0:T(8,128)(2,1)S(1)}, bf16[32,1024]{1,0:T(8,128)(2,1)}, u32[]{:S(2)}) copy-start(bf16[32,1024]{1,0:T(8,128)(2,1)} %param.26) | copy-start | bytes 196612
  61.8 10.9 %all-to-all-start.1 = ((f32[32,2,8]{2,1,0:T(2,128)}), f32[32,2,8]{2,1,0:T(2,128)S(1)}, u32[]{:S(2)}, u32[]{:S(2)}) async-start(f32[32,2,8]{2,1,0:T(2,128)} %copy.104), calls=%async_computation.1 | async-start | bytes 65536 | tf_op jit(solution)/shard_map/all_to_all | solution.py:107
  66.0 105.4 %copy-start.5 = (f32[1024]{0:T(1024)S(1)}, f32[1024]{0:T(1024)}, u32[]{:S(2)}) copy-start(f32[1024]{0:T(1024)} %param.27) | copy-start | bytes 12292
  72.7 11.7 %all-to-all-start = ((f32[32,2,8,128]{3,2,1,0:T(8,128)}), f32[32,2,8,128]{3,2,1,0:T(8,128)S(1)}, u32[]{:S(2)}, u32[]{:S(2)}) async-start(f32[32,2,8,128]{3,2,1,0:T(8,128)} %copy.103), calls=%async_computation | async-start | bytes 524288 | tf_op jit(solution)/shard_map/all_to_all | solution.py:109
  76.1 73.0 %all-reduce.4.cloned.1.call-start = ((), (), s32[]{:S(2)}) async-start(), calls=%async_computation.4 | async-start | bytes 131072 | tf_op jit(solution)/shard_map/psum | solution.py:147
  119.0 142.8 %all-reduce.6.cloned.1.call-start = ((), (), s32[]{:S(2)}) async-start(), calls=%async_computation.6 | async-start | bytes 1835008 | tf_op jit(solution)/shard_map/psum | solution.py:159
  171.4 8.7 %copy-start.3 = (bf16[32,1024]{1,0:T(8,128)(2,1)S(1)}, bf16[32,1024]{1,0:T(8,128)(2,1)}, u32[]{:S(2)}) copy-start(bf16[32,1024]{1,0:T(8,128)(2,1)} %all-reduce.4.cloned.1.call-done) | copy-start | bytes 196612
  188.7 100.7 %reduce-scatter.2.cloned.1.call-start = ((), (), s32[]{:S(2)}) async-start(), calls=%async_computation.5 | async-start | bytes 81920 | tf_op jit(solution)/shard_map/reduce_scatter | solution.py:165
Sparse Core Ops, SparseCore 0:
  119.1 29.9 all-reduce.3
  188.9 72.9 all-reduce.5
  270.7 18.6 reduce-scatter.1
where the time goes:
time: 298 us; the launch traced here: 297 us
  waiting for transfers between devices  137 us (46%)
  blocking collectives  84.5 us (28%)
  matrix products  38 us (13%)
  between operations  13.3 us (4%)
  starting transfers between devices  13.1 us (4%)
  local copies, waits for them, and re-layouts  5.71 us (2%)
  other arithmetic  5.33 us (2%)
    psum x1, waiting for transfers between devices, on_device(): lax.psum(jnp.dot(normed, up_weight, preferred_element_type=jnp.float32).a...  73.1 us
    all_gather x1, blocking collectives, on_device(): gathered = lax.all_gather(queries, 'node', axis=0, tiled=True)  32.5 us
    all_gather x1, blocking collectives, on_device(): lax.all_gather(attended, 'node', axis=0, tiled=True)  30.6 us
    psum x1, waiting for transfers between devices, on_device(): lax.psum(projected.astype(jnp.bfloat16), 'mp').astype(jnp.float32)  30 us
    psum x1, blocking collectives, on_device(): squares = lax.psum(jnp.sum(stream * stream, axis=1), 'node')  21.4 us
    reduce_scatter x1, waiting for transfers between devices, on_device(): lax.psum_scatter(jnp.dot(act, down_weight, preferred_element_type=jnp.flo...  18.8 us
    dot_general x1, matrix products, on_device(): jnp.dot(act, down_weight, preferred_element_type=jnp.float32)  8.71 us
    dot_general x1, matrix products, on_device(): jnp.dot(normed, up_weight, preferred_element_type=jnp.float32)  8.67 us
  transfers between devices with their start and end apart: 6, of which 6 were waited for; matrix products, arithmetic and copies ran while one was open for 2% of the time, Pallas kernels for 0%

commit v1 on v0

--- a/solution.py
+++ b/solution.py
@@ -61,7 +61,14 @@
     group_size = local_heads // local_groups
     scaling = head_size ** (-0.5)
     node_count = lax.axis_size("node")
-    gathered = lax.all_gather(queries, "node", axis=0, tiled=True)
+    n_dev = lax.axis_size("node")
+    route = [(i, (i + 1) % n_dev) for i in range(n_dev)]
+    terms = [queries]
+    for hop in range(1, n_dev):
+        terms = [lax.ppermute(terms[0], "node", route), *terms]
+    full = jnp.concatenate(terms, axis=0)
+    shift = (lax.axis_index("node") + 1) * terms[-1].shape[0]
+    gathered = jnp.roll(full, shift, axis=0)
     every_branch = gathered.shape[0]
     grouped = gathered.reshape(every_branch, local_groups, group_size, head_size)
     root_usable = jnp.ones((every_branch, root_keys.shape[0]), dtype=bool)

time: 298 us -> 308 us (1.034)
  waiting for transfers between devices: 137 us -> 174 us
  blocking collectives: 84.5 us -> 51.9 us
    ppermute x0 -> x7, waiting for transfers between devices: none -> 38.6 us  [on_device(): terms = [lax.ppermute(terms[0], 'node', route), *terms]]
    all_gather x1 -> x0, blocking collectives: 32.5 us -> none  [on_device(): gathered = lax.all_gather(queries, 'node', axis=0, tiled=True)]
  transfers between devices with their start and end apart: 6 -> 13, of which waited for: 6 -> 13; matrix products, arithmetic and copies ran while one was open for 2% -> 4% of each run, Pallas kernels for 0% -> 0%
where the time goes in v1:
time: 308 us; the launch traced here: 307 us
  waiting for transfers between devices  174 us (56%)
  blocking collectives  51.9 us (17%)
  matrix products  40.4 us (13%)
  between operations  13.4 us (4%)
  starting transfers between devices  13.2 us (4%)
  other arithmetic  8.14 us (3%)
  local copies, waits for them, and re-layouts  5.56 us (2%)
    psum x1, waiting for transfers between devices, on_device(): lax.psum(jnp.dot(normed, up_weight, preferred_element_type=jnp.float32).a...  73.2 us
    ppermute x7, waiting for transfers between devices, on_device(): terms = [lax.ppermute(terms[0], 'node', route), *terms]  38.6 us
    all_gather x1, blocking collectives, on_device(): lax.all_gather(attended, 'node', axis=0, tiled=True)  30.5 us
    psum x1, waiting for transfers between devices, on_device(): lax.psum(projected.astype(jnp.bfloat16), 'mp').astype(jnp.float32)  30.2 us
    psum x1, blocking collectives, on_device(): squares = lax.psum(jnp.sum(stream * stream, axis=1), 'node')  21.4 us
    reduce_scatter x1, waiting for transfers between devices, on_device(): lax.psum_scatter(jnp.dot(act, down_weight, preferred_element_type=jnp.flo...  18.8 us
    dot_general x1, matrix products, on_device(): jnp.dot(act, down_weight, preferred_element_type=jnp.float32)  8.71 us
    dot_general x1, matrix products, on_device(): jnp.dot(normed, up_weight, preferred_element_type=jnp.float32)  8.67 us
  transfers between devices with their start and end apart: 13, of which 13 were waited for; matrix products, arithmetic and copies ran while one was open for 4% of the time, Pallas kernels for 0%

profile of v1, /device:TPU:0, one launch (start us, length us, event | category | flops | bytes accessed | tf_op | source)
XLA Modules:
  0.0 306.9 jit_solution(13024679936554392162)
XLA Ops:
  6.5 3.0 collective-permute-start
  9.5 0.7 iota_compare_fusion
  10.2 4.2 %collective-permute-done = bf16[4,16,128]{2,1,0:T(8,128)(2,1)S(1)} collective-permute-done((bf16[4,16,128]{2,1,0:T(8,128)(2,1)}, bf16[4,16,128]{2,1,0:T(8,128)(2,1)S(1)}, u32[]{:S(2)}, u32[]{:S(2)}) %collective-permute-start) | collective-permute-done | bytes 16416 | tf_op jit(solution)/shard_map/ppermute | solution.py:68
  14.5 1.4 fusion.85
  15.9 5.0 %collective-permute-done.1 = bf16[4,16,128]{2,1,0:T(8,128)(2,1)S(1)} collective-permute-done((bf16[4,16,128]{2,1,0:T(8,128)(2,1)S(1)}, bf16[4,16,128]{2,1,0:T(8,128)(2,1)S(1)}, u32[]{:S(2)}, u32[]{:S(2)}) %collective-permute-start.1) | collective-permute-done | bytes 16416 | tf_op jit(solution)/shard_map/ppermute | solution.py:68
  20.9 0.7 compare_bitcast_fusion
  21.6 0.1 copy.110
  21.7 0.1 reduce-window.7
  21.7 5.6 %collective-permute-done.2 = bf16[4,16,128]{2,1,0:T(8,128)(2,1)S(1)} collective-permute-done((bf16[4,16,128]{2,1,0:T(8,128)(2,1)S(1)}, bf16[4,16,128]{2,1,0:T(8,128)(2,1)S(1)}, u32[]{:S(2)}, u32[]{:S(2)}) %collective-permute-start.2) | collective-permute-done | bytes 16416 | tf_op jit(solution)/shard_map/ppermute | solution.py:68
  27.3 0.1 add_reduce_fusion
  27.5 6.3 %collective-permute-done.3 = bf16[4,16,128]{2,1,0:T(8,128)(2,1)S(1)} collective-permute-done((bf16[4,16,128]{2,1,0:T(8,128)(2,1)S(1)}, bf16[4,16,128]{2,1,0:T(8,128)(2,1)S(1)}, u32[]{:S(2)}, u32[]{:S(2)}) %collective-permute-start.3) | collective-permute-done | bytes 16416 | tf_op jit(solution)/shard_map/ppermute | solution.py:68
  33.8 6.4 %collective-permute-done.4 = bf16[4,16,128]{2,1,0:T(8,128)(2,1)S(1)} collective-permute-done((bf16[4,16,128]{2,1,0:T(8,128)(2,1)S(1)}, bf16[4,16,128]{2,1,0:T(8,128)(2,1)S(1)}, u32[]{:S(2)}, u32[]{:S(2)}) %collective-permute-start.4) | collective-permute-done | bytes 16416 | tf_op jit(solution)/shard_map/ppermute | solution.py:68
  40.2 1.2 dynamic_slice.23
  41.5 5.2 %collective-permute-done.5 = bf16[4,16,128]{2,1,0:T(8,128)(2,1)S(1)} collective-permute-done((bf16[4,16,128]{2,1,0:T(8,128)(2,1)S(1)}, bf16[4,16,128]{2,1,0:T(8,128)(2,1)S(1)}, u32[]{:S(2)}, u32[]{:S(2)}) %collective-permute-start.5) | collective-permute-done | bytes 16416 | tf_op jit(solution)/shard_map/ppermute | solution.py:68
  46.7 0.7 iota_compare_fusion.2
  47.3 5.8 %collective-permute-done.6 = bf16[4,16,128]{2,1,0:T(8,128)(2,1)S(1)} collective-permute-done((bf16[4,16,128]{2,1,0:T(8,128)(2,1)S(1)}, bf16[4,16,128]{2,1,0:T(8,128)(2,1)S(1)}, u32[]{:S(2)}, u32[]{:S(2)}) %collective-permute-start.6) | collective-permute-done | bytes 16416 | tf_op jit(solution)/shard_map/ppermute | solution.py:68
  53.2 0.7 constant_dynamic-update-slice_fusion.8
  54.0 0.7 constant_dynamic-update-slice_fusion
  54.7 0.1 convolution_convert_fusion.4
  54.8 1.4 fusion.84
  56.3 0.1 copy.114
  56.3 0.2 fusion.39
  56.6 1.3 convolution_bitcast_fusion
  57.9 0.1 copy.134
  58.0 0.3 fusion.48
  58.3 0.0 copy-start.4
  58.3 2.6 bitcast_reduce_fusion
  61.0 0.1 copy.116
  61.0 0.1 subtract_exponential_fusion.2
  61.2 0.7 copy.123
  61.9 3.3 %all-to-all-start.1 = ((f32[32,2,8]{2,1,0:T(2,128)}), f32[32,2,8]{2,1,0:T(2,128)S(1)}, u32[]{:S(2)}, u32[]{:S(2)}) async-start(f32[32,2,8]{2,1,0:T(2,128)} %copy.123), calls=%async_computation.1 | async-start | bytes 65536 | tf_op jit(solution)/shard_map/all_to_all | solution.py:114
  65.2 3.0 fusion.1
  68.2 0.1 copy.133
  68.3 0.1 fusion.24
  68.4 0.1 copy.120
  68.5 0.1 copy.117
  68.6 0.7 copy.135
  69.3 2.6 all-to-all-done.1
  71.9 3.4 %all-to-all-start.2 = ((f32[32,2,8]{2,1,0:T(2,128)}), f32[32,2,8]{2,1,0:T(2,128)S(1)}, u32[]{:S(2)}, u32[]{:S(2)}) async-start(f32[32,2,8]{2,1,0:T(2,128)} %copy.135), calls=%async_computation.2 | async-start | bytes 65536 | tf_op jit(solution)/shard_map/all_to_all | solution.py:115
  75.2 3.1 %fusion.15 = f32[32,2,8,128]{3,2,0,1:T(8,128)S(1)} fusion(f32[2,32,8,2048]{3,2,1,0:T(8,128)} %get-tuple-element.49, f32[32,2,8]{2,0,1:T(8,128)S(1)} %get-tuple-element.48, bf16[2048,2,128,1]{2,1,0,3:T(2,128)(2,1)S(1)} %bitcast.84, f32[32,2,8,128]{3,0,2,1:T(8,128)S(1)} %fusion.48, f32[32,2,8]{2,0,1:T(8,128)S(1)} %copy.120, f32[32,2,8]{2,0,1:T(8,128)S(1)} %copy.117), kind=kOutput, calls=%fused_computation.15 | convolution fusion | flops 271777792 | bytes 5773312 | tf_op jit(solution)/shard_map/bkgl,lkd->bkgd/dot_general | solution.py:21
  78.3 0.7 copy.122
  79.1 3.0 all-to-all-done.2
  82.0 3.4 %all-to-all-start = ((f32[32,2,8,128]{3,2,1,0:T(8,128)}), f32[32,2,8,128]{3,2,1,0:T(8,128)S(1)}, u32[]{:S(2)}, u32[]{:S(2)}) async-start(f32[32,2,8,128]{3,2,1,0:T(8,128)} %copy.122), calls=%async_computation | async-start | bytes 524288 | tf_op jit(solution)/shard_map/all_to_all | solution.py:116
  85.5 0.0 all-reduce.4.cloned.1.call-start
  85.5 0.2 fusion.50
  85.8 7.9 %all-to-all-done = f32[32,2,8,128]{3,2,1,0:T(8,128)S(1)} async-done(((f32[32,2,8,128]{3,2,1,0:T(8,128)}), f32[32,2,8,128]{3,2,1,0:T(8,128)S(1)}, u32[]{:S(2)}, u32[]{:S(2)}) %all-to-all-start) | async-done | bytes 262176 | tf_op jit(solution)/shard_map/all_to_all | solution.py:116
  93.7 0.1 fusion.42
  93.9 0.2 fusion.21
  94.1 30.5 %all-gather = bf16[8,4,2048]{2,1,0:T(4,128)(2,1)S(1)} all-gather(bf16[1,4,2048]{2,1,0:T(4,128)(2,1)S(1)} %reshape.273), channel_id=1, replica_groups=mesh['node'=8,'mp'=4] {'node'}, dimensions={0}, use_global_device_ids=true | all-gather | bytes 147456 | tf_op jit(solution)/shard_map/all_gather | solution.py:150
  124.7 3.6 %convolution_convert_fusion.3 = bf16[32,1024]{1,0:T(8,128)(2,1)} fusion(bf16[32,2048]{1,0:T(8,128)(2,1)S(1)} %reshape.274, bf16[2048,1024]{1,0:T(8,128)(2,1)} %param.28), kind=kOutput, calls=%fused_computation.19 | convolution fusion | flops 134250496 | bytes 4390912 | tf_op jit(solution)/shard_map/dot_general | solution.py:149
  128.3 0.0 all-reduce.4.cloned.1.call-update
  128.4 0.0 all-reduce.6.cloned.1.call-start
  128.4 30.2 %all-reduce.4.cloned.1.call-done = bf16[32,1024]{1,0:T(8,128)(2,1)} async-done(((bf16[32,1024]{1,0:T(8,128)(2,1)}), bf16[32,1024]{1,0:T(8,128)(2,1)}) %all-reduce.4.cloned.1.call-update) | async-done | bytes 65552 | tf_op jit(solution)/shard_map/psum | solution.py:154
  158.6 1.0 convert_add_fusion
  159.6 21.4 %psum.29 = f32[32]{0:T(128)S(1)} all-reduce(f32[32]{0:T(128)S(1)} %get-tuple-element.45), channel_id=1, replica_groups=mesh['node'=8,'mp'=4] {'node'}, use_global_device_ids=true, to_apply=%region_13.14 | all-reduce | flops 32 | bytes 256 | tf_op jit(solution)/shard_map/psum | solution.py:156
  181.0 8.7 %convolution_convert_fusion = bf16[32,7168]{1,0:T(8,128)(2,1)} fusion(bf16[1024,7168]{1,0:T(8,128)(2,1)} %param.30, f32[1024]{0:T(1024)S(1)} %copy-done.3, f32[32]{0:T(128)S(1)} %add_rsqrt_fusion, bf16[32,1024]{1,0:T(8,128)(2,1)} %all-reduce.4.cloned.1.call-done, bf16[32,1024]{1,0:T(8,128)(2,1)S(1)} %copy-done.1), kind=kOutput, calls=%fused_computation | convolution fusion | flops 470188032 | bytes 15274112 | tf_op jit(solution)/shard_map/dot_general | solution.py:167
  189.6 8.6 %convolution_convert_fusion.1 = bf16[32,7168]{1,0:T(8,128)(2,1)} fusion(bf16[1024,7168]{1,0:T(8,128)(2,1)} %param.29, f32[1024]{0:T(1024)S(1)} %copy-done.3, f32[32]{0:T(128)S(1)} %add_rsqrt_fusion, bf16[32,1024]{1,0:T(8,128)(2,1)S(1)} %copy-done.2, bf16[32,1024]{1,0:T(8,128)(2,1)S(1)} %copy-done.1), kind=kOutput, calls=%fused_computation.1 | convolution fusion | flops 470188032 | bytes 15274112 | tf_op jit(solution)/shard_map/dot_general | solution.py:163
  198.3 0.0 all-reduce.6.cloned.1.call-update
  198.3 0.0 reduce-scatter.2.cloned.1.call-start
  198.3 73.2 %all-reduce.6.cloned.1.call-done = (bf16[32,7168]{1,0:T(8,128)(2,1)}, bf16[32,7168]{1,0:T(8,128)(2,1)}) async-done(((bf16[32,7168]{1,0:T(8,128)(2,1)}, bf16[32,7168]{1,0:T(8,128)(2,1)}), (bf16[32,7168]{1,0:T(8,128)(2,1)}, bf16[32,7168]{1,0:T(8,128)(2,1)})) %all-reduce.6.cloned.1.call-update) | async-done | bytes 917520 | tf_op jit(solution)/shard_map/psum | solution.py:166
  271.5 8.7 %convolution_convert_fusion.2 = bf16[32,1024]{1,0:T(8,128)(2,1)} fusion(bf16[7168,1024]{1,0:T(8,128)(2,1)} %param.31, bf16[32,7168]{1,0:T(8,128)(2,1)} %get-tuple-element.23, bf16[32,7168]{1,0:T(8,128)(2,1)} %get-tuple-element.24), kind=kOutput, calls=%fused_computation.18 | convolution fusion | flops 471629824 | bytes 15663104 | tf_op jit(solution)/shard_map/dot_general | solution.py:173
  280.2 0.0 reduce-scatter.2.cloned.1.call-update
  280.2 18.8 %reduce-scatter.2.cloned.1.call-done = bf16[8,1024]{1,0:T(8,128)(2,1)} async-done(((bf16[32,1024]{1,0:T(8,128)(2,1)}), bf16[8,1024]{1,0:T(8,128)(2,1)}) %reduce-scatter.2.cloned.1.call-update) | async-done | bytes 16400 | tf_op jit(solution)/shard_map/reduce_scatter | solution.py:172
  299.1 1.3 add_convert_fusion
  (46 shorter events, 0.3 us)
Async XLA Ops:
  6.5 51.8 %copy-start = (bf16[2048,2,128]{2,1,0:T(2,128)(2,1)S(1)}, bf16[2048,2,128]{2,1,0:T(2,128)(2,1)}, u32[]{:S(2)}) copy-start(bf16[2048,2,128]{2,1,0:T(2,128)(2,1)} %param.17) | copy-start | bytes 3145732
  6.5 7.9 %collective-permute-start = (bf16[4,16,128]{2,1,0:T(8,128)(2,1)}, bf16[4,16,128]{2,1,0:T(8,128)(2,1)S(1)}, u32[]{:S(2)}, u32[]{:S(2)}) collective-permute-start(bf16[4,16,128]{2,1,0:T(8,128)(2,1)} %param.16), channel_id=1, source_target_pairs={{0,4},{4,8},{8,12},{12,16},{16,20},{20,24},{24,28},{28,0},{1,5},{5... | collective-permute-start | bytes 49160 | tf_op jit(solution)/shard_map/ppermute | solution.py:68
  14.5 6.4 %collective-permute-start.1 = (bf16[4,16,128]{2,1,0:T(8,128)(2,1)S(1)}, bf16[4,16,128]{2,1,0:T(8,128)(2,1)S(1)}, u32[]{:S(2)}, u32[]{:S(2)}) collective-permute-start(bf16[4,16,128]{2,1,0:T(8,128)(2,1)S(1)} %collective-permute-done), channel_id=1, source_target_pairs={{0,4},{4,8},{8,12},{12,16},{16,20},{20,24},{24,28},{28,0},{1,5},{5... | collective-permute-start | bytes 49160 | tf_op jit(solution)/shard_map/ppermute | solution.py:68
  20.9 6.4 %collective-permute-start.2 = (bf16[4,16,128]{2,1,0:T(8,128)(2,1)S(1)}, bf16[4,16,128]{2,1,0:T(8,128)(2,1)S(1)}, u32[]{:S(2)}, u32[]{:S(2)}) collective-permute-start(bf16[4,16,128]{2,1,0:T(8,128)(2,1)S(1)} %collective-permute-done.1), channel_id=1, source_target_pairs={{0,4},{4,8},{8,12},{12,16},{16,20},{20,24},{24,28},{28,0},{1,5},{5... | collective-permute-start | bytes 49160 | tf_op jit(solution)/shard_map/ppermute | solution.py:68
  27.3 6.4 %collective-permute-start.3 = (bf16[4,16,128]{2,1,0:T(8,128)(2,1)S(1)}, bf16[4,16,128]{2,1,0:T(8,128)(2,1)S(1)}, u32[]{:S(2)}, u32[]{:S(2)}) collective-permute-start(bf16[4,16,128]{2,1,0:T(8,128)(2,1)S(1)} %collective-permute-done.2), channel_id=1, source_target_pairs={{0,4},{4,8},{8,12},{12,16},{16,20},{20,24},{24,28},{28,0},{1,5},{5... | collective-permute-start | bytes 49160 | tf_op jit(solution)/shard_map/ppermute | solution.py:68
  33.8 6.4 %collective-permute-start.4 = (bf16[4,16,128]{2,1,0:T(8,128)(2,1)S(1)}, bf16[4,16,128]{2,1,0:T(8,128)(2,1)S(1)}, u32[]{:S(2)}, u32[]{:S(2)}) collective-permute-start(bf16[4,16,128]{2,1,0:T(8,128)(2,1)S(1)} %collective-permute-done.3), channel_id=1, source_target_pairs={{0,4},{4,8},{8,12},{12,16},{16,20},{20,24},{24,28},{28,0},{1,5},{5... | collective-permute-start | bytes 49160 | tf_op jit(solution)/shard_map/ppermute | solution.py:68
  40.2 6.4 %collective-permute-start.5 = (bf16[4,16,128]{2,1,0:T(8,128)(2,1)S(1)}, bf16[4,16,128]{2,1,0:T(8,128)(2,1)S(1)}, u32[]{:S(2)}, u32[]{:S(2)}) collective-permute-start(bf16[4,16,128]{2,1,0:T(8,128)(2,1)S(1)} %collective-permute-done.4), channel_id=1, source_target_pairs={{0,4},{4,8},{8,12},{12,16},{16,20},{20,24},{24,28},{28,0},{1,5},{5... | collective-permute-start | bytes 49160 | tf_op jit(solution)/shard_map/ppermute | solution.py:68
  46.7 6.4 %collective-permute-start.6 = (bf16[4,16,128]{2,1,0:T(8,128)(2,1)S(1)}, bf16[4,16,128]{2,1,0:T(8,128)(2,1)S(1)}, u32[]{:S(2)}, u32[]{:S(2)}) collective-permute-start(bf16[4,16,128]{2,1,0:T(8,128)(2,1)S(1)} %collective-permute-done.5), channel_id=1, source_target_pairs={{0,4},{4,8},{8,12},{12,16},{16,20},{20,24},{24,28},{28,0},{1,5},{5... | collective-permute-start | bytes 49160 | tf_op jit(solution)/shard_map/ppermute | solution.py:68
  58.3 16.9 %copy-start.4 = (bf16[2048,2,128]{2,1,0:T(2,128)(2,1)S(1)}, bf16[2048,2,128]{2,1,0:T(2,128)(2,1)}, u32[]{:S(2)}) copy-start(bf16[2048,2,128]{2,1,0:T(2,128)(2,1)} %param.18) | copy-start | bytes 3145732
  61.9 10.0 %all-to-all-start.1 = ((f32[32,2,8]{2,1,0:T(2,128)}), f32[32,2,8]{2,1,0:T(2,128)S(1)}, u32[]{:S(2)}, u32[]{:S(2)}) async-start(f32[32,2,8]{2,1,0:T(2,128)} %copy.123), calls=%async_computation.1 | async-start | bytes 65536 | tf_op jit(solution)/shard_map/all_to_all | solution.py:114
  68.2 25.6 %copy-start.5 = (bf16[4,256,2,128]{3,2,1,0:T(2,128)(2,1)S(1)}, bf16[4,256,2,128]{3,2,1,0:T(2,128)(2,1)}, u32[]{:S(2)}) copy-start(bf16[4,256,2,128]{3,2,1,0:T(2,128)(2,1)} %param.22) | copy-start | bytes 1572868
  71.9 10.2 %all-to-all-start.2 = ((f32[32,2,8]{2,1,0:T(2,128)}), f32[32,2,8]{2,1,0:T(2,128)S(1)}, u32[]{:S(2)}, u32[]{:S(2)}) async-start(f32[32,2,8]{2,1,0:T(2,128)} %copy.135), calls=%async_computation.2 | async-start | bytes 65536 | tf_op jit(solution)/shard_map/all_to_all | solution.py:115
  78.3 80.3 %copy-start.1 = (bf16[32,1024]{1,0:T(8,128)(2,1)S(1)}, bf16[32,1024]{1,0:T(8,128)(2,1)}, u32[]{:S(2)}) copy-start(bf16[32,1024]{1,0:T(8,128)(2,1)} %param.26) | copy-start | bytes 196612
  78.3 102.6 %copy-start.3 = (f32[1024]{0:T(1024)S(1)}, f32[1024]{0:T(1024)}, u32[]{:S(2)}) copy-start(f32[1024]{0:T(1024)} %param.27) | copy-start | bytes 12292
  82.0 11.7 %all-to-all-start = ((f32[32,2,8,128]{3,2,1,0:T(8,128)}), f32[32,2,8,128]{3,2,1,0:T(8,128)S(1)}, u32[]{:S(2)}, u32[]{:S(2)}) async-start(f32[32,2,8,128]{3,2,1,0:T(8,128)} %copy.122), calls=%async_computation | async-start | bytes 524288 | tf_op jit(solution)/shard_map/all_to_all | solution.py:116
  85.5 73.2 %all-reduce.4.cloned.1.call-start = ((), (), s32[]{:S(2)}) async-start(), calls=%async_computation.4 | async-start | bytes 131072 | tf_op jit(solution)/shard_map/psum | solution.py:154
  128.4 143.2 %all-reduce.6.cloned.1.call-start = ((), (), s32[]{:S(2)}) async-start(), calls=%async_computation.6 | async-start | bytes 1835008 | tf_op jit(solution)/shard_map/psum | solution.py:166
  181.0 8.7 %copy-start.2 = (bf16[32,1024]{1,0:T(8,128)(2,1)S(1)}, bf16[32,1024]{1,0:T(8,128)(2,1)}, u32[]{:S(2)}) copy-start(bf16[32,1024]{1,0:T(8,128)(2,1)} %all-reduce.4.cloned.1.call-done) | copy-start | bytes 196612
  198.3 100.8 %reduce-scatter.2.cloned.1.call-start = ((), (), s32[]{:S(2)}) async-start(), calls=%async_computation.5 | async-start | bytes 81920 | tf_op jit(solution)/shard_map/reduce_scatter | solution.py:172
Sparse Core Ops, SparseCore 0:
  128.5 30.1 all-reduce.3
  198.4 73.0 all-reduce.5
  280.4 18.6 reduce-scatter.1
